TPU v7x, 256 devices: a whole 4x4x8 slice. The times are simulated.
256 devices in a mesh: seq: 64 (over z, y, core), chan: 4 (over x).
Axes of the slice: x: 4, y: 4, z: 8, core: 2. Of those that a mesh axis runs over, the one named last changes fastest.
Arguments:
- signal: bfloat16 [16384, 2048], P('seq', 'chan'), may hold values from -6 to 6
- gate_rows: bfloat16 [16384, 2048], P('seq', 'chan'), may hold values from -60 to 60
- skip_gain: float32 [2048], P('chan'), may hold values from 0.5 to 1.5
- filter_taps: bfloat16 [16384, 16], P(None, 'chan'), may hold values from -2 to 2
- queries: bfloat16 [16384, 2048], P('seq', 'chan'), may hold values from -6 to 6
- key_rows: bfloat16 [16384, 2048], P('seq', 'chan'), may hold values from -6 to 6
Outputs:
- conv_mixed: bfloat16 [16384, 2048], P('seq', 'chan')
- attended: bfloat16 [256, 1024, 128], P(('chan', 'seq'))
All inputs are finite; a program needn't handle non-finite values.
Results may differ from a plain program's by a relative error of at most 0.0061.
Values may be sent and summed in bfloat16 or wider, within the bound.
A program may use at most 128 MiB of HBM per device.

v0:
```python
import math

import jax
import jax.numpy as jnp
from jax import lax
from jax.sharding import PartitionSpec as P


def toeplitz_block(padded_taps, out_start, in_start, block_rows, group_rows, seq_len):
    heads_loc = padded_taps.shape[0]
    window_len = group_rows + block_rows - 1
    offset = out_start - in_start - block_rows + 1 + seq_len
    window = lax.dynamic_slice_in_dim(padded_taps, offset, window_len, 1)
    flipped = jnp.concatenate(
        [window[:, ::-1], jnp.zeros((heads_loc, 1), padded_taps.dtype)], axis=1
    )
    repeated = jnp.tile(flipped, (1, group_rows))[:, : group_rows * window_len]
    return repeated.reshape(heads_loc, group_rows, window_len)[:, :, group_rows - 1 :]


def add_range(total_acc, inputs, first_row, target, lower, upper, padded_taps, seq_len, head_dim):
    block_rows = inputs.shape[0]
    group_rows = total_acc.shape[0]
    positions = first_row + jnp.arange(block_rows, dtype=jnp.int32)
    keep_rows = (positions >= lower) & (positions < upper)
    is_live = (first_row < upper) & (first_row + block_rows > lower)

    def compute(running):
        masked = jnp.where(keep_rows[:, None], inputs, jnp.zeros_like(inputs))
        matrix = toeplitz_block(padded_taps, target, first_row, block_rows, group_rows, seq_len)
        heads_loc = matrix.shape[0]
        split_in = masked.reshape(block_rows, heads_loc, head_dim)
        product = jnp.einsum("htn,nhd->thd", matrix, split_in, preferred_element_type=jnp.float32)
        return running + product.reshape(group_rows, heads_loc * head_dim)

    def unchanged(running):
        return running

    return lax.cond(is_live, compute, unchanged, total_acc)


def attend_block(q_rows, q_pos, key_end, keys_all, values_all, score_scale):
    key_part = keys_all[:key_end]
    value_part = values_all[:key_end]
    raw_scores = (
        jnp.einsum("qd,kd->qk", q_rows, key_part, preferred_element_type=jnp.float32) * score_scale
    )
    k_pos = jnp.arange(key_end, dtype=jnp.int32)
    masked = jnp.where(k_pos[None, :] <= q_pos[:, None], raw_scores, -jnp.inf)
    peak = jnp.max(masked, axis=1)
    exp_scores = jnp.exp(masked - peak[:, None])
    row_total = jnp.sum(exp_scores, axis=1)
    weighted = jnp.dot(
        exp_scores.astype(jnp.bfloat16), value_part, preferred_element_type=jnp.float32
    )
    return (weighted / row_total[:, None]).astype(jnp.bfloat16)


def shards(signal, gate_rows, skip_gain, filter_taps, queries, key_rows):
    group_rows, local_width = signal.shape
    heads_loc = filter_taps.shape[1]
    head_dim = local_width // heads_loc
    seq_count = lax.axis_size("seq")
    chan_count = lax.axis_size("chan")
    my_group = lax.axis_index("seq")
    seq_len = group_rows * seq_count
    padded_taps = jnp.concatenate(
        [jnp.zeros((seq_len, heads_loc), filter_taps.dtype), filter_taps], axis=0
    ).T
    own_start = my_group * group_rows
    own_upper = own_start + group_rows
    halfway = seq_count // 2
    own_lower = jnp.zeros((), jnp.int32)
    help_upper = jnp.zeros((), jnp.int32)
    help_start = (my_group + halfway) % seq_count * group_rows

    def add_both(totals, inputs, first_row):
        own_acc = add_range(
            totals[0],
            inputs,
            first_row,
            own_start,
            own_lower,
            own_upper,
            padded_taps,
            seq_len,
            head_dim,
        )
        help_acc = add_range(
            totals[1], inputs, first_row, help_start, 0, help_upper, padded_taps, seq_len, head_dim
        )
        return (own_acc, help_acc)

    zero_acc = jnp.zeros((group_rows, local_width), jnp.float32)
    totals = (zero_acc, zero_acc)
    incoming = lax.all_gather(signal, "seq", axis=0, tiled=True)
    incoming_rows = incoming.shape[0]
    pieces_count = incoming_rows // group_rows
    blocks = incoming.reshape(pieces_count, group_rows, local_width)
    starts = group_rows * jnp.arange(pieces_count, dtype=jnp.int32)

    def step_block(running, entry_pair):
        return (add_both(running, entry_pair[0], entry_pair[1]), None)

    totals, unused = lax.scan(step_block, totals, (blocks, starts))
    own_acc, help_acc = totals
    conv_mixed = (
        gate_rows.astype(jnp.float32) * (own_acc + skip_gain[None, :] * signal.astype(jnp.float32))
    ).astype(jnp.bfloat16)
    widened = conv_mixed.astype(jnp.float32)
    squares = jnp.sum(jnp.square(widened), axis=1)
    whole_sum = lax.psum(squares, "chan")
    inv_scale = lax.rsqrt(whole_sum / (local_width * chan_count) + 1e-06)
    values = (widened * inv_scale[:, None]).astype(jnp.bfloat16)
    query_sets = seq_count // heads_loc
    query_rows = group_rows // query_sets
    query_send = (
        queries.reshape(query_sets, query_rows, heads_loc, head_dim)
        .transpose(2, 0, 1, 3)
        .reshape(seq_count, query_rows, head_dim)
    )
    pair_stack = jnp.concatenate(
        [
            key_rows.reshape(group_rows, heads_loc, head_dim),
            values.reshape(group_rows, heads_loc, head_dim),
        ],
        axis=2,
    ).transpose(1, 0, 2)
    pair_send = jnp.broadcast_to(
        pair_stack[:, None], (heads_loc, query_sets, group_rows, 2 * head_dim)
    ).reshape(seq_count, group_rows, 2 * head_dim)
    query_got, pair_got = (
        lax.all_to_all(query_send, "seq", split_axis=0, concat_axis=1, tiled=True),
        lax.all_to_all(pair_send, "seq", split_axis=0, concat_axis=1, tiled=True),
    )
    query_all = query_got[0]
    keys_all = pair_got[0, :, :head_dim]
    values_all = pair_got[0, :, head_dim:]
    my_set = my_group % query_sets
    query_len = query_all.shape[0]
    query_block = min(512, query_len)
    score_scale = 1.0 / math.sqrt(head_dim)
    outputs = []
    for query_step in range(query_len // query_block):
        local_index = query_step * query_block + jnp.arange(query_block, dtype=jnp.int32)
        q_pos = (
            local_index // query_rows * group_rows + my_set * query_rows + local_index % query_rows
        )
        last_source = ((query_step + 1) * query_block - 1) // query_rows
        key_end = (last_source + 1) * group_rows
        q_rows = query_all[query_step * query_block : (query_step + 1) * query_block]
        outputs.append(attend_block(q_rows, q_pos, key_end, keys_all, values_all, score_scale))
    attended = jnp.concatenate(outputs, axis=0)[None]
    return (conv_mixed, attended)


def solution(mesh):
    in_specs = (
        P("seq", "chan"),
        P("seq", "chan"),
        P("chan"),
        P(None, "chan"),
        P("seq", "chan"),
        P("seq", "chan"),
    )
    out_specs = (P("seq", "chan"), P(("chan", "seq"), None, None))
    return jax.shard_map(shards, mesh=mesh, in_specs=in_specs, out_specs=out_specs, check_vma=False)
```

profile of v0, /device:TPU:1, one launch (start us, length us, event | category | flops | bytes accessed | tf_op | source)
XLA Modules:
  0.0 986.5 jit_solution(6087917328609244170)
XLA Ops:
  7.2 0.7 all-gather.2.cloned.1.call-update
  7.9 1.0 reshape.122
  8.9 0.7 copy.16
  9.7 13.1 %all-to-all-start.1 = ((bf16[64,16,128]{2,1,0:T(8,128)(2,1)}), bf16[64,16,128]{2,1,0:T(8,128)(2,1)S(1)}, u32[]{:S(2)}, u32[]{:S(2)}) async-start(bf16[64,16,128]{2,1,0:T(8,128)(2,1)} %bitcast.11), calls=%async_computation.1 | async-start | bytes 524288 | tf_op jit(solution)/shard_map/all_to_all | solution.py:133
  22.8 1.7 reshape.119
  24.5 1.7 pad_bitcast_fusion
  26.2 88.0 %all-gather.2.cloned.1.call-done = bf16[16384,512]{1,0:T(8,128)(2,1)} async-done(((bf16[256,512]{1,0:T(8,128)(2,1)}), bf16[16384,512]{1,0:T(8,128)(2,1)}) %all-gather.2.cloned.1.call-update) | async-done | bytes 16777232 | tf_op jit(solution)/shard_map/all_gather | solution.py:96
  114.3 22.3 %copy.13 = bf16[64,256,512]{1,2,0:T(8,128)(2,1)} copy(bf16[64,256,512]{2,1,0:T(8,128)(2,1)} %bitcast.58) | data formatting | bytes 33554432 | tf_op jit(solution)/shard_map/while | solution.py:105
  136.7 135.4 %while.13 = (s32[]{:T(128)}, f32[256,512]{0,1:T(8,128)S(1)}, s32[64]{0:T(128)S(1)}, s32[]{:T(128)}, bf16[64,256,512]{1,2,0:T(8,128)(2,1)}, /*index=5*/s32[]{:T(1...) while((s32[]{:T(128)}, f32[256,512]{0,1:T(8,128)S(1)}, s32[64]{0:T(128)S(1)}, s32[]{:T(128)}, ...), condition=%wide.region_3.4_spmd, body=%wide.region_0.3_spmd.sunk | while | flops 67372048 | bytes 10779659 | solution.py:105
  136.7 0.6 dynamic_slice.18
  138.5 7.0 conditional.2
  139.8 0.8 constant_dynamic-slice_fusion
  141.0 1.0 constant_dynamic-slice_fusion.1
  142.1 0.8 copy.17
  143.3 1.8 reshape.110
  145.5 0.6 dynamic_slice.18
  147.4 7.0 conditional.2
  148.7 0.8 constant_dynamic-slice_fusion
  149.9 1.0 constant_dynamic-slice_fusion.1
  151.0 0.8 copy.17
  152.1 1.8 reshape.110
  158.2 0.6 dynamic_slice.18
  160.1 0.6 dynamic_slice.18
  163.9 0.6 dynamic_slice.18
  165.8 0.6 dynamic_slice.18
  167.7 0.6 dynamic_slice.18
  171.5 0.6 dynamic_slice.18
  173.4 0.6 dynamic_slice.18
  175.3 0.6 dynamic_slice.18
  179.1 0.6 dynamic_slice.18
  181.0 0.6 dynamic_slice.18
  182.9 0.6 dynamic_slice.18
  186.7 0.6 dynamic_slice.18
  188.6 0.6 dynamic_slice.18
  194.3 0.6 dynamic_slice.18
  196.2 0.6 dynamic_slice.18
  200.0 0.6 dynamic_slice.18
  201.9 0.6 dynamic_slice.18
  203.8 0.6 dynamic_slice.18
  207.6 0.6 dynamic_slice.18
  209.5 0.6 dynamic_slice.18
  211.4 0.6 dynamic_slice.18
  215.2 0.6 dynamic_slice.18
  217.1 0.6 dynamic_slice.18
  219.0 0.6 dynamic_slice.18
  222.8 0.6 dynamic_slice.18
  224.6 0.6 dynamic_slice.18
  230.3 0.6 dynamic_slice.18
  232.2 0.6 dynamic_slice.18
  236.0 0.6 dynamic_slice.18
  237.9 0.6 dynamic_slice.18
  272.3 1.2 fusion.28
  273.5 8.4 psum.7
  282.1 1.2 maximum_bitcast_fusion
  283.4 4.2 broadcast_in_dim.23
  287.6 436.4 %all-to-all-start = ((bf16[64,256,256]{2,1,0:T(8,128)(2,1)}), bf16[64,256,256]{2,1,0:T(8,128)(2,1)}, u32[]{:S(2)}, u32[]{:S(2)}) async-start(bf16[64,256,256]{2,1,0:T(8,128)(2,1)} %bitcast.56), calls=%async_computation | async-start | bytes 16777216 | tf_op jit(solution)/shard_map/all_to_all | solution.py:134
  724.1 182.3 %all-to-all-done = bf16[64,256,256]{2,1,0:T(8,128)(2,1)} async-done(((bf16[64,256,256]{2,1,0:T(8,128)(2,1)}), bf16[64,256,256]{2,1,0:T(8,128)(2,1)}, u32[]{:S(2)}, u32[]{:S(2)}) %all-to-all-start) | async-done | bytes 8388640 | tf_op jit(solution)/shard_map/all_to_all | solution.py:134
  906.4 9.2 fusion.47
  915.6 8.0 fusion.11
  923.6 8.8 fusion.25
  932.5 16.5 %fusion.46 = (f32[512]{0:T(512)S(1)}, f32[512,16384]{0,1:T(8,128)}) fusion(bf16[512,128]{1,0:T(8,128)(2,1)S(1)} %bitcast.61, bf16[1,16384,256]{2,1,0:T(8,128)(2,1)} %bitcast.8, s32[512]{0:T(512)S(1)} %get-tuple-element.138), kind=kOutput, calls=%fused_computation.70 | convolution fusion | flops 2181037568 | bytes 37883904 | tf_op jit(solution)/shard_map/qd,kd->qk/dot_general | solution.py:46
  949.0 15.0 %fusion.6 = f32[512]{0:T(512)S(1)} fusion(f32[512,16384]{0,1:T(8,128)} %get-tuple-element.134, f32[512]{0:T(512)S(1)} %get-tuple-element.133), kind=kLoop, calls=%fused_computation.14 | loop fusion | flops 16776704 | bytes 33558528 | tf_op jit(solution)/shard_map/reduce_sum | solution.py:52
  964.0 14.9 %fusion.19 = bf16[512,128]{1,0:T(8,128)(2,1)S(1)} fusion(bf16[1,16384,256]{2,1,0:T(8,128)(2,1)} %bitcast.8, f32[512,16384]{0,1:T(8,128)} %get-tuple-element.134, f32[512]{0:T(512)S(1)} %get-tuple-element.133, f32[512]{0:T(512)S(1)} %fusion.6), kind=kOutput, calls=%fused_computation.30 | convolution fusion | flops 2164391936 | bytes 37883904 | tf_op jit(solution)/shard_map/dot_general | solution.py:53
  978.9 0.7 maximum_bitcast_fusion.1
  (191 shorter events, 25.4 us)
Async XLA Ops:
  7.2 107.1 %all-gather.2.cloned.1.call-start = ((), (), s32[]{:S(2)}) async-start(), calls=%async_computation.2 | async-start | bytes 17039360 | tf_op jit(solution)/shard_map/all_gather | solution.py:96
  9.7 273.7 %all-to-all-start.1 = ((bf16[64,16,128]{2,1,0:T(8,128)(2,1)}), bf16[64,16,128]{2,1,0:T(8,128)(2,1)S(1)}, u32[]{:S(2)}, u32[]{:S(2)}) async-start(bf16[64,16,128]{2,1,0:T(8,128)(2,1)} %bitcast.11), calls=%async_computation.1 | async-start | bytes 524288 | tf_op jit(solution)/shard_map/all_to_all | solution.py:133
  136.6 135.7 %copy-start = (bf16[256,512]{1,0:T(8,128)(2,1)S(1)}, bf16[256,512]{1,0:T(8,128)(2,1)}, u32[]{:S(2)}) copy-start(bf16[256,512]{1,0:T(8,128)(2,1)} %param.10) | copy-start | bytes 786436
  136.6 135.7 %copy-start.2 = (f32[512]{0:T(512)S(1)}, f32[512]{0:T(512)}, u32[]{:S(2)}) copy-start(f32[512]{0:T(512)} %param.12) | copy-start | bytes 6148
  273.5 642.2 %copy-start.1 = (bf16[256,512]{1,0:T(8,128)(2,1)}, bf16[256,512]{1,0:T(8,128)(2,1)S(1)}, u32[]{:S(2)}) copy-start(bf16[256,512]{1,0:T(8,128)(2,1)S(1)} %get-tuple-element.130) | copy-start | bytes 786436
  287.6 618.8 %all-to-all-start = ((bf16[64,256,256]{2,1,0:T(8,128)(2,1)}), bf16[64,256,256]{2,1,0:T(8,128)(2,1)}, u32[]{:S(2)}, u32[]{:S(2)}) async-start(bf16[64,256,256]{2,1,0:T(8,128)(2,1)} %bitcast.56), calls=%async_computation | async-start | bytes 16777216 | tf_op jit(solution)/shard_map/all_to_all | solution.py:134
Sparse Core Ops, SparseCore 0:
  10.7 103.4 all-gather.1
where the time goes:
time: 997 us; the launch traced here: 986 us
  starting transfers between devices  450 us (45%)
  waiting for transfers between devices  271 us (27%)
  loops' own time  83 us (8%)
  local copies, waits for them, and re-layouts  82.4 us (8%)
  matrix products  50.2 us (5%)
  other arithmetic  27.7 us (3%)
  between operations  14.2 us (1%)
    all_to_all x1, starting transfers between devices, shards(): lax.all_to_all(pair_send, 'seq', split_axis=0, concat_axis=1, tiled=True)  436 us
    all_to_all x1, waiting for transfers between devices, shards(): lax.all_to_all(pair_send, 'seq', split_axis=0, concat_axis=1, tiled=True)  182 us
    all_gather x1, waiting for transfers between devices, shards(): incoming = lax.all_gather(signal, 'seq', axis=0, tiled=True)  88 us
    another operation x1, loops' own time, shards(): totals, unused = lax.scan(step_block, totals, (blocks, starts))  80.7 us
    dynamic_slice x66, local copies, waits for them, and re-layouts, shards(): totals, unused = lax.scan(step_block, totals, (blocks, starts))  41.6 us
    dot_general x2, matrix products, attend_block(): jnp.einsum('qd,kd->qk', q_rows, key_part, preferred_element_type=jnp.floa...  25.7 us
    dot_general x2, matrix products, attend_block(): jnp.dot(exp_scores.astype(jnp.bfloat16), value_part, preferred_element_ty...  23.7 us
    reduce_sum x2, other arithmetic, attend_block(): row_total = jnp.sum(exp_scores, axis=1)  23.1 us
  transfers between devices with their start and end apart: 3, of which 2 were waited for; matrix products, arithmetic and copies ran while one was open for 8% of the time, Pallas kernels for 0%

commit v1 on v0

v1 whole, which is shorter than its diff:
```python
import math

import jax
import jax.numpy as jnp
from jax import lax
from jax.experimental import pallas as pl
from jax.experimental.pallas import tpu as pltpu
from jax.sharding import PartitionSpec as P

ROWS = 256
BLOCKS = 64
HD = 128
SETS = 16
QR = 16
CH = 8
LANE = 128
F32 = jnp.float32
BF16 = jnp.bfloat16
VMEM = pl.BlockSpec(memory_space=pltpu.VMEM)


def fill_toeplitz(taps_ref, gg_ref):
    row = lax.broadcasted_iota(jnp.int32, (LANE, LANE), 0)
    lane = lax.broadcasted_iota(jnp.int32, (LANE, LANE), 1)
    mask = lane >= row

    def rotated(chunk):
        line = jnp.broadcast_to(taps_ref[pl.ds(chunk, 1), :], (LANE, LANE))
        return pltpu.roll(line, 0, 1, stride=1, stride_axis=0)

    def body(d, carry):
        before, tile_before = carry
        first = rotated(2 * d)
        tile_a = jnp.where(mask, first, before).astype(BF16)
        second = rotated(2 * d + 1)
        tile_b = jnp.where(mask, second, first).astype(BF16)
        top = pl.ds(pl.multiple_of(d * 256, 256), LANE)
        low = pl.ds(pl.multiple_of(d * 256 + LANE, LANE), LANE)
        gg_ref[top, :LANE] = tile_a
        gg_ref[top, LANE:] = tile_b
        gg_ref[low, :LANE] = tile_before
        gg_ref[low, LANE:] = tile_a
        return second, tile_b

    lax.fori_loop(
        0, BLOCKS, body, (jnp.zeros((LANE, LANE), F32), jnp.zeros((LANE, LANE), BF16))
    )


def conv_kernel(taps_ref, sg_ref, skip_ref, cm_ref, gg_ref, xf_ref, xx_ref, acc_ref):
    fill_toeplitz(taps_ref, gg_ref)
    xf_ref[:64, :] = jnp.zeros((64, ROWS), F32)
    xf_ref[64:, :] = sg_ref[:, 0].astype(F32).reshape(BLOCKS * CH, ROWS)
    for e in range(8):
        xx_ref[:, e * ROWS : (e + 1) * ROWS] = xf_ref[64 - 8 * e : 576 - 8 * e, :].astype(BF16)
    acc_ref[...] = jnp.dot(xx_ref[...], gg_ref[:2048, :], preferred_element_type=F32)
    for g in range(1, 8):
        acc_ref[64 * g :, :] += jnp.dot(
            xx_ref[: 512 - 64 * g, :],
            gg_ref[2048 * g : 2048 * (g + 1), :],
            preferred_element_type=F32,
        )
    conv = acc_ref[...].reshape(BLOCKS, CH, ROWS)
    sig = sg_ref[:, 0].astype(F32)
    gate = sg_ref[:, 1].astype(F32)
    cm_ref[...] = (gate * (conv + skip_ref[...][None] * sig)).astype(BF16)


def conv_call(taps, sg, skip):
    return pl.pallas_call(
        conv_kernel,
        out_shape=jax.ShapeDtypeStruct((BLOCKS, CH, ROWS), BF16),
        in_specs=[VMEM] * 3,
        out_specs=VMEM,
        scratch_shapes=[
            pltpu.VMEM((BLOCKS * ROWS, ROWS), BF16),
            pltpu.VMEM((576, ROWS), F32),
            pltpu.VMEM((512, 2048), BF16),
            pltpu.VMEM((512, ROWS), F32),
        ],
        compiler_params=pltpu.CompilerParams(vmem_limit_bytes=50 * 2**20),
        name="conv",
    )(taps, sg, skip)


def score_tile(q_ref, k_ref, s_ref, t, my_set):
    qt = q_ref[256 * t : 256 * (t + 1), :].astype(F32).T.astype(BF16)
    qt_hi = qt[:, LANE:]

    def keys(i):
        return k_ref[:, i].reshape(ROWS, HD)

    def fold(s):
        return jnp.max(s.reshape(ROWS // 8, 8, s.shape[1]), axis=0)

    def plain(i, m):
        s = jnp.dot(keys(i), qt, preferred_element_type=F32)
        s_ref[i] = s
        return jnp.maximum(m, fold(s))

    def masked(i, width, lane0):
        s = jnp.dot(keys(i), qt if width == 256 else qt_hi, preferred_element_type=F32)
        lanes = lax.broadcasted_iota(jnp.int32, (ROWS, width), 1) + lane0
        rows = lax.broadcasted_iota(jnp.int32, (ROWS, width), 0)
        q_pos = (16 * t + lanes // QR) * ROWS + my_set * QR + lanes % QR
        return jnp.where(rows + i * ROWS <= q_pos, s, -jnp.inf)

    def diag(i, m):
        s = masked(i, 256, 0)
        s_ref[i] = s
        return jnp.maximum(m, fold(s))

    def diag_hi(i, m):
        s = masked(i, LANE, LANE)
        s_ref[i, :, LANE:] = s
        return jnp.maximum(m, fold(s))

    m = jnp.full((8, 256), -jnp.inf, F32)
    if t > 0:
        m = lax.fori_loop(0, 16 * t, plain, m, unroll=2)
    m = lax.fori_loop(16 * t, 16 * t + 8, diag, m, unroll=2)
    m_hi = lax.fori_loop(16 * t + 8, 16 * t + 16, diag_hi, m[:, LANE:], unroll=2)
    m = jnp.concatenate([m[:, :LANE], m_hi], axis=1)
    return jnp.max(m, axis=0, keepdims=True)


def attend_kernel(q_ref, k_ref, v_ref, inv_ref, out_ref, s_ref, vt_ref):
    my_set = lax.rem(lax.axis_index("seq"), SETS)
    factor = (1.0 / math.sqrt(HD)) * math.log2(math.e)

    def scale(i, carry):
        v = v_ref[:, i].astype(F32).reshape(HD, ROWS)
        vt_ref[i] = (v * inv_ref[pl.ds(i, 1), :]).astype(BF16)
        return carry

    lax.fori_loop(0, BLOCKS, scale, 0, unroll=2)
    for t in range(4):
        peak = score_tile(q_ref, k_ref, s_ref, t, my_set)

        def weigh(i, carry, wide=True):
            acc, total = carry
            s = s_ref[i] if wide else s_ref[i, :, LANE:]
            p = jnp.exp2((s - (peak if wide else peak[:, LANE:])) * factor)
            total = total + jnp.sum(p.reshape(ROWS // 8, 8, p.shape[1]), axis=0)
            acc = acc + jnp.dot(vt_ref[i], p.astype(BF16), preferred_element_type=F32)
            return acc, total

        acc, total = lax.fori_loop(
            0,
            16 * t + 8,
            weigh,
            (jnp.zeros((HD, 256), F32), jnp.zeros((8, 256), F32)),
            unroll=2,
        )
        acc_hi, total_hi = lax.fori_loop(
            16 * t + 8,
            16 * t + 16,
            lambda i, c: weigh(i, c, False),
            (acc[:, LANE:], total[:, LANE:]),
            unroll=2,
        )
        acc = jnp.concatenate([acc[:, :LANE], acc_hi], axis=1)
        total = jnp.concatenate([total[:, :LANE], total_hi], axis=1)
        total = jnp.sum(total, axis=0, keepdims=True)
        out_ref[256 * t : 256 * (t + 1), :] = (acc / total).T.astype(BF16)


def attend_call(q, k, v, inv):
    return pl.pallas_call(
        attend_kernel,
        out_shape=jax.ShapeDtypeStruct((BLOCKS * QR, HD), BF16),
        in_specs=[VMEM] * 4,
        out_specs=VMEM,
        scratch_shapes=[
            pltpu.VMEM((BLOCKS, ROWS, 256), F32),
            pltpu.VMEM((BLOCKS, HD, ROWS), BF16),
        ],
        compiler_params=pltpu.CompilerParams(vmem_limit_bytes=50 * 2**20),
        name="attend",
    )(q, k, v, inv)


def shards(signal, gate_rows, skip_gain, filter_taps, queries, key_rows):
    me = lax.axis_index("seq")
    head = me // SETS
    heads_loc = filter_taps.shape[1]
    groups = [[h * SETS + b for b in range(SETS)] for h in range(heads_loc)]

    def split_rows(x):
        return (
            x.reshape(SETS, QR, heads_loc, HD).transpose(2, 0, 1, 3).reshape(BLOCKS, 1, QR, HD)
        )

    def split_channels(x):
        return x.T.reshape(BLOCKS, 1, CH, ROWS)

    sg = jnp.concatenate([split_channels(signal), split_channels(gate_rows)], axis=1)
    qk = jnp.concatenate([split_rows(queries), split_rows(key_rows)], axis=1)
    sg = lax.all_to_all(sg, "seq", split_axis=0, concat_axis=0, tiled=True)
    qk = lax.all_to_all(qk, "seq", split_axis=0, concat_axis=0, tiled=True)
    k_all = lax.all_gather(qk[:, 1], "seq", axis=0, tiled=False, axis_index_groups=groups)
    taps = lax.dynamic_slice_in_dim(filter_taps.T, head, 1, 0).reshape(LANE, LANE).astype(F32)
    skip = jnp.broadcast_to(lax.dynamic_slice_in_dim(skip_gain, me * CH, CH)[:, None], (CH, ROWS))
    cm = conv_call(taps, sg, skip)
    cm_all = lax.all_gather(cm, "seq", axis=0, tiled=False, axis_index_groups=groups)
    home = lax.all_to_all(cm, "seq", split_axis=0, concat_axis=0, tiled=True)
    home = home.reshape(BLOCKS * CH, ROWS)
    squares = jnp.sum(jnp.square(home.astype(F32)), axis=0)
    whole = lax.psum(squares, "chan")
    inv = lax.rsqrt(whole / (heads_loc * HD * lax.axis_size("chan")) + 1e-06)
    inv_all = lax.all_gather(inv, "seq", axis=0, tiled=False)
    attended = attend_call(qk[:, 0].reshape(BLOCKS * QR, HD), k_all, cm_all, inv_all)
    return home.T, attended[None]


def solution(mesh):
    in_specs = (
        P("seq", "chan"),
        P("seq", "chan"),
        P("chan"),
        P(None, "chan"),
        P("seq", "chan"),
        P("seq", "chan"),
    )
    out_specs = (P("seq", "chan"), P(("chan", "seq"), None, None))
    return jax.shard_map(shards, mesh=mesh, in_specs=in_specs, out_specs=out_specs, check_vma=False)
```

time: 997 us -> 203 us (0.20); the launches traced: 986 us -> 203 us
  starting transfers between devices: 450 us -> 13.2 us
  waiting for transfers between devices: 271 us -> 15.9 us
  blocking collectives: 8.41 us -> 101 us
  loops' own time: 83 us -> 0 us
  local copies, waits for them, and re-layouts: 82.4 us -> 4.87 us
  Pallas kernels: 0 us -> 51.3 us
  matrix products: 50.2 us -> 0 us
  other arithmetic: 27.7 us -> 1.97 us
    all_to_all x2 -> x1, starting transfers between devices: 450 us -> 13.1 us  [shards(): sg = lax.all_to_all(sg, 'seq', split_axis=0, concat_axis=0, tiled=True)]
    all_to_all x2 -> x1, waiting for transfers between devices: 182 us -> 15.9 us  [shards(): sg = lax.all_to_all(sg, 'seq', split_axis=0, concat_axis=0, tiled=True)]
    all_gather x1 -> x2, waiting for transfers between devices: 88 us -> 0.01 us  [the longest x1 0.01 us: shards(): lax.all_gather(cm, 'seq', axis=0, tiled=False, axis_index_groups=groups)]
    another operation x65 -> x0, loops' own time: 83 us -> none  [the longest x1 80.7 us: shards(): totals, unused = lax.scan(step_block, totals, (blocks, starts))]
    pallas_call x0 -> x2, Pallas kernels: none -> 51.3 us  [the longest x1 40.8 us: attend_call(): pl.pallas_call(attend_kernel, out_shape=jax.ShapeDtypeStruct((BLOCKS * QR...]
    dot_general x6 -> x0, matrix products: 50.2 us -> none  [the longest x2 25.7 us: attend_block(): jnp.einsum('qd,kd->qk', q_rows, key_part, preferred_element_type=jnp.floa...]
    all_to_all x0 -> x2, blocking collectives: none -> 47.2 us  [the longest x1 25.7 us: shards(): qk = lax.all_to_all(qk, 'seq', split_axis=0, concat_axis=0, tiled=True)]
    all_gather x0 -> x1, blocking collectives: none -> 45.6 us  [shards(): inv_all = lax.all_gather(inv, 'seq', axis=0, tiled=False)]
  transfers between devices with their start and end apart: 3 -> 3, of which waited for: 2 -> 1; matrix products, arithmetic and copies ran while one was open for 8% -> 2% of each run, Pallas kernels for 0% -> 0%
where the time goes in v1:
time: 203 us
  blocking collectives  101 us (50%)
  Pallas kernels  51.3 us (25%)
  waiting for transfers between devices  15.9 us (8%)
  between operations  14.1 us (7%)
  starting transfers between devices  13.2 us (7%)
  local copies, waits for them, and re-layouts  4.87 us (2%)
    all_gather x1, blocking collectives, shards(): inv_all = lax.all_gather(inv, 'seq', axis=0, tiled=False)  45.6 us
    pallas_call x1, Pallas kernels, attend_call(): pl.pallas_call(attend_kernel, out_shape=jax.ShapeDtypeStruct((BLOCKS * QR...  40.8 us
    all_to_all x1, blocking collectives, shards(): qk = lax.all_to_all(qk, 'seq', split_axis=0, concat_axis=0, tiled=True)  25.7 us
    all_to_all x1, blocking collectives, shards(): home = lax.all_to_all(cm, 'seq', split_axis=0, concat_axis=0, tiled=True)  21.5 us
    all_to_all x1, waiting for transfers between devices, shards(): sg = lax.all_to_all(sg, 'seq', split_axis=0, concat_axis=0, tiled=True)  15.9 us
    all_to_all x1, starting transfers between devices, shards(): sg = lax.all_to_all(sg, 'seq', split_axis=0, concat_axis=0, tiled=True)  13.1 us
    pallas_call x1, Pallas kernels, conv_call(): pl.pallas_call(conv_kernel, out_shape=jax.ShapeDtypeStruct((BLOCKS, CH, R...  10.5 us
    psum x1, blocking collectives, shards(): whole = lax.psum(squares, 'chan')  8.58 us
  transfers between devices with their start and end apart: 3, of which 1 were waited for; matrix products, arithmetic and copies ran while one was open for 2% of the time, Pallas kernels for 0%

profile of v1, /device:TPU:1, one launch (start us, length us, event | category | flops | bytes accessed | tf_op | source)
XLA Modules:
  0.0 202.9 jit_solution(12693148929566927243)
XLA Ops:
  7.2 0.0 copy-start
  7.2 0.0 copy-start.1
  7.2 1.1 copy.13
  8.3 1.1 copy.14
  9.4 0.8 pad_maximum_fusion
  10.3 13.1 %all-to-all-start = ((bf16[64,2,8,256]{3,2,1,0:T(8,128)(2,1)}), bf16[64,2,8,256]{3,2,1,0:T(8,128)(2,1)S(1)}, u32[]{:S(2)}, u32[]{:S(2)}) async-start(bf16[64,2,8,256]{3,2,1,0:T(8,128)(2,1)} %pad_maximum_fusion), calls=%async_computation | async-start | bytes 1048576 | tf_op jit(solution)/shard_map/all_to_all | solution.py:199
  23.4 0.0 all-gather.9.cloned.1.call-start
  23.5 0.8 dynamic_slice.4
  24.2 1.0 dynamic-slice_convert_fusion
  25.2 15.9 %all-to-all-done.sg_ref = bf16[64,2,8,256]{3,2,1,0:T(8,128)(2,1)S(1)} async-done(((bf16[64,2,8,256]{3,2,1,0:T(8,128)(2,1)}), bf16[64,2,8,256]{3,2,1,0:T(8,128)(2,1)S(1)}, u32[]{:S(2)}, u32[]{:S(2)}) %all-to-all-start) | async-done | bytes 524320 | tf_op jit(solution)/shard_map/all_to_all | solution.py:199
  41.1 0.1 broadcast_in_dim.4.skip_ref
  41.2 10.5 %conv.1 = bf16[64,8,256]{2,1,0:T(8,128)(2,1)} custom-call(f32[128,128]{1,0:T(8,128)S(1)} %bitcast.23, bf16[64,2,8,256]{3,2,1,0:T(8,128)(2,1)S(1)} %all-to-all-done.sg_ref, f32[8,256]{1,0:T(8,128)S(1)} %broadcast_in_dim.4.skip_ref), custom_call_target="tpu_custom_call" | custom-call | tf_op jit(solution)/shard_map/conv/pallas_call | solution.py:70
  51.7 0.0 all-gather.9.cloned.1.call-update
  51.7 0.0 all-gather.7.cloned.1.call-start
  51.7 0.0 copy-done
  51.7 0.1 reshape.34
  51.9 0.0 copy-done.1
  51.9 0.1 reshape.36
  52.0 0.1 pad_maximum_fusion.1
  52.0 25.7 %all_to_all.15 = bf16[64,2,16,128]{3,2,1,0:T(8,128)(2,1)S(1)} all-to-all(bf16[64,2,16,128]{3,2,1,0:T(8,128)(2,1)S(1)} %pad_maximum_fusion.1), channel_id=1, replica_groups=mesh['seq'=64,'chan'=4] {'seq'}, dimensions={0} | all-to-all | bytes 1048576 | tf_op jit(solution)/shard_map/all_to_all | solution.py:200
  77.8 0.8 fusion
  78.5 0.0 all-gather.7.cloned.1.call-update
  78.5 21.5 %all_to_all.16 = bf16[64,8,256]{2,1,0:T(8,128)(2,1)S(1)} all-to-all(bf16[64,8,256]{2,1,0:T(8,128)(2,1)} %conv.1), channel_id=1, replica_groups=mesh['seq'=64,'chan'=4] {'seq'}, dimensions={0} | all-to-all | bytes 524288 | tf_op jit(solution)/shard_map/all_to_all | solution.py:206
  100.1 0.1 multiply_reduce_fusion
  100.2 8.6 %psum.7 = f32[256]{0:T(256)S(1)} all-reduce(f32[256]{0:T(256)S(1)} %multiply_reduce_fusion), channel_id=1, replica_groups=mesh['seq'=64,'chan'=4] {'chan'}, use_global_device_ids=true, to_apply=%region_1.2 | all-reduce | flops 256 | bytes 2048 | tf_op jit(solution)/shard_map/psum | solution.py:209
  108.7 45.6 %all-gather.3 = f32[64,1,256]{2,1,0:T(1,128)S(1)} all-gather(f32[1,1,256]{2,1,0:T(1,128)S(1)} %bitcast.35), channel_id=4, replica_groups=mesh['seq'=64,'chan'=4] {'seq'}, dimensions={0}, use_global_device_ids=true | all-gather | bytes 66560 | tf_op jit(solution)/shard_map/all_gather | solution.py:211
  154.3 0.8 copy.15
  155.2 0.0 all-gather.9.cloned.1.call-done
  155.2 0.0 all-gather.7.cloned.1.call-done
  155.2 40.8 %attend.1 = bf16[1024,128]{1,0:T(8,128)(2,1)} custom-call(bf16[1024,128]{1,0:T(8,128)(2,1)S(1)} %bitcast.21, bf16[16,64,16,128]{3,2,1,0:T(8,128)(2,1)} %bitcast.25, bf16[16,64,8,256]{3,2,1,0:T(8,128)(2,1)} %bitcast.24, f32[64,256]{1,0:T(8,128)S(1)} %bitcast.22), custom_call_target="tpu_custom_call" | custom-call | tf_op jit(solution)/shard_map/attend/pallas_call | solution.py:169
  (4 shorter events, 0.1 us)
Async XLA Ops:
  7.2 44.6 %copy-start = (bf16[256,512]{1,0:T(8,128)(2,1)S(1)}, bf16[256,512]{1,0:T(8,128)(2,1)}, u32[]{:S(2)}) copy-start(bf16[256,512]{1,0:T(8,128)(2,1)} %param.10) | copy-start | bytes 786436
  7.2 44.7 %copy-start.1 = (bf16[256,512]{1,0:T(8,128)(2,1)S(1)}, bf16[256,512]{1,0:T(8,128)(2,1)}, u32[]{:S(2)}) copy-start(bf16[256,512]{1,0:T(8,128)(2,1)} %param.11) | copy-start | bytes 786436
  10.3 30.8 %all-to-all-start = ((bf16[64,2,8,256]{3,2,1,0:T(8,128)(2,1)}), bf16[64,2,8,256]{3,2,1,0:T(8,128)(2,1)S(1)}, u32[]{:S(2)}, u32[]{:S(2)}) async-start(bf16[64,2,8,256]{3,2,1,0:T(8,128)(2,1)} %pad_maximum_fusion), calls=%async_computation | async-start | bytes 1048576 | tf_op jit(solution)/shard_map/all_to_all | solution.py:199
  23.4 131.8 %all-gather.9.cloned.1.call-start = ((), (), s32[]{:S(2)}) async-start(), calls=%async_computation.4 | async-start | bytes 4456448 | tf_op jit(solution)/shard_map/all_gather | solution.py:205
  51.7 103.5 %all-gather.7.cloned.1.call-start = ((), (), s32[]{:S(2)}) async-start(), calls=%async_computation.3 | async-start | bytes 4456448 | tf_op jit(solution)/shard_map/all_gather | solution.py:201
Sparse Core Ops, SparseCore 0:
  51.8 47.0 all-gather.8
  100.8 41.7 all-gather.6

commit v2 on v1

v2 whole, which is shorter than its diff:
```python
import math

import jax
import jax.numpy as jnp
from jax import lax
from jax.experimental import pallas as pl
from jax.experimental.pallas import tpu as pltpu
from jax.sharding import PartitionSpec as P

ROWS = 256
BLOCKS = 64
HD = 128
SETS = 16
QR = 16
CH = 8
LANE = 128
F32 = jnp.float32
BF16 = jnp.bfloat16
MESH = pl.DeviceIdType.MESH
VMEM = pl.BlockSpec(memory_space=pltpu.VMEM)


def fill_toeplitz(taps_ref, gg_ref):
    row = lax.broadcasted_iota(jnp.int32, (LANE, LANE), 0)
    lane = lax.broadcasted_iota(jnp.int32, (LANE, LANE), 1)
    mask = lane >= row

    def rotated(chunk):
        line = jnp.broadcast_to(taps_ref[pl.ds(chunk, 1), :], (LANE, LANE))
        return pltpu.roll(line, 0, 1, stride=1, stride_axis=0)

    def body(d, carry):
        before, tile_before = carry
        first = rotated(2 * d)
        tile_a = jnp.where(mask, first, before).astype(BF16)
        second = rotated(2 * d + 1)
        tile_b = jnp.where(mask, second, first).astype(BF16)
        top = pl.ds(pl.multiple_of(d * 256, 256), LANE)
        low = pl.ds(pl.multiple_of(d * 256 + LANE, LANE), LANE)
        gg_ref[top, :LANE] = tile_a
        gg_ref[top, LANE:] = tile_b
        gg_ref[low, :LANE] = tile_before
        gg_ref[low, LANE:] = tile_a
        return second, tile_b

    lax.fori_loop(
        0, BLOCKS, body, (jnp.zeros((LANE, LANE), F32), jnp.zeros((LANE, LANE), BF16))
    )


def landed(ref, sem):
    pltpu.make_async_copy(ref, ref, sem).wait()


def fold_rows(x, op):
    return op(x.reshape(x.shape[0] // 8, 8, x.shape[1]), axis=0)


def tile_base(slot, t):
    return slot * 80 + 4 * t * (t + 1)


def mega_kernel(
    sig_ref, gate_ref, taps_ref, skip_ref, q_ref, k_ref,
    mixed_ref, out_ref,
    st_s, st_g, rs, rg, qb, kb, cmh, hb, vb, sq_out, sq_in, inv_out, inv_in,
    gg, xf, xx, acc_ref, s_ref, p_ref, vt_ref, stat, ob_out, ob_in, os_out, os_in,
    a_send, a_recv, k_send, k_recv, v_send, v_recv, o_send, o_recv,
):
    seq_count = lax.axis_size("seq")
    chan_count = lax.axis_size("chan")
    me = lax.axis_index("seq")
    my_chan = lax.axis_index("chan")
    core = me % 2
    y = (me // 2) % 4
    row0 = (me // 8) * 8
    zr = (me // 8) % 2
    my_set = me % SETS
    my_slot = me % 8
    other_core = me + 1 - 2 * core
    across = me + 8 - 16 * zr
    row1 = row0 + 8 - 16 * zr
    factor = (1.0 / math.sqrt(HD)) * math.log2(math.e)

    def send(src, dst, s_sem, r_sem, where):
        pltpu.make_async_remote_copy(
            src_ref=src, dst_ref=dst, send_sem=s_sem, recv_sem=r_sem,
            device_id=where, device_id_type=MESH,
        ).start()

    def others(body):
        def step(n, carry):
            body((me + n) % seq_count)
            return carry

        lax.fori_loop(1, seq_count, step, 0)

    def piece(ref, d):
        rows = pl.ds(pl.multiple_of((d % SETS) * QR, QR), QR)
        return ref.at[rows, pl.ds(pl.multiple_of((d // SETS) * HD, HD), HD)]

    def flip(d):
        return d + 8 - 16 * ((d // 8) % 2)

    st_s[...] = sig_ref[...].astype(F32).T.reshape(BLOCKS, CH, ROWS).astype(BF16)
    st_g[...] = gate_ref[...].astype(F32).T.reshape(BLOCKS, CH, ROWS).astype(BF16)

    barrier = pltpu.get_barrier_semaphore()
    others(
        lambda d: pl.semaphore_signal(
            barrier, inc=1, device_id={"seq": d}, device_id_type=MESH
        )
    )
    for n in range(1, chan_count):
        pl.semaphore_signal(
            barrier, inc=1, device_id={"chan": (my_chan + n) % chan_count}, device_id_type=MESH
        )
    pl.semaphore_wait(barrier, seq_count + chan_count - 2)

    others(lambda d: send(st_s.at[d], rs.at[me], a_send.at[0], a_recv.at[0], {"seq": d}))
    others(
        lambda d: send(
            piece(k_ref, d), kb.at[d % 8, me], a_send.at[1], a_recv.at[1], {"seq": d}
        )
    )
    others(lambda d: send(st_g.at[d], rg.at[me], a_send.at[2], a_recv.at[2], {"seq": d}))

    def send_queries(d):
        send(piece(q_ref, flip(d)), qb.at[1, me], a_send.at[3], a_recv.at[3], {"seq": d})
        send(piece(q_ref, d), qb.at[0, me], a_send.at[4], a_recv.at[4], {"seq": d})

    others(send_queries)
    rs[me] = st_s[me]
    rg[me] = st_g[me]
    kb[my_slot, me] = piece(k_ref, me)[...]
    qb[0, me] = piece(q_ref, me)[...]
    qb[1, me] = piece(q_ref, across)[...]

    fill_toeplitz(taps_ref, gg)
    xf[:64, :] = jnp.zeros((64, ROWS), F32)
    landed(rs.at[pl.ds(0, 63)], a_recv.at[0])
    xf[64:, :] = rs[...].astype(F32).reshape(BLOCKS * CH, ROWS)
    for e in range(8):
        xx[:, e * ROWS : (e + 1) * ROWS] = xf[64 - 8 * e : 576 - 8 * e, :].astype(BF16)
    acc_ref[...] = jnp.dot(xx[...], gg[:2048, :], preferred_element_type=F32)
    for g in range(1, 8):
        acc_ref[64 * g :, :] += jnp.dot(
            xx[: 512 - 64 * g, :],
            gg[2048 * g : 2048 * (g + 1), :],
            preferred_element_type=F32,
        )

    landed(kb.at[0, pl.ds(0, 63)], a_recv.at[1])
    row_mates = [row0 + ((y + n) % 4) * 2 + core for n in range(4)]
    far_mates = [row1 + ((y + n) % 4) * 2 + core for n in range(4)]
    for n in (1, 3, 2):
        send(
            kb.at[my_slot], kb.at[my_slot], k_send.at[n], k_recv.at[my_slot],
            {"seq": row_mates[n]},
        )
    send(kb.at[my_slot], kb.at[my_slot], k_send.at[0], k_recv.at[my_slot], {"seq": other_core})

    landed(rg.at[pl.ds(0, 63)], a_recv.at[2])
    conv = acc_ref[...].reshape(BLOCKS, CH, ROWS)
    mixed = rg[...].astype(F32) * (conv + skip_ref[...][None] * rs[...].astype(F32))
    mixed = mixed.astype(BF16)
    cmh[0] = mixed[:, :, :LANE]
    cmh[1] = mixed[:, :, LANE:]
    others(lambda d: send(cmh.at[:, d], hb.at[me], a_send.at[5], a_recv.at[5], {"seq": d}))
    hb[me] = cmh[:, me]
    vb[my_set] = cmh[zr]
    for n in range(4):
        where = other_core if n == 0 else row_mates[n]
        send(cmh.at[zr], vb.at[my_set], v_send.at[n], v_recv.at[my_set], {"seq": where})
    for n in range(4):
        send(
            cmh.at[1 - zr], vb.at[my_set], v_send.at[4 + n], v_recv.at[my_set],
            {"seq": far_mates[n]},
        )

    landed(hb.at[pl.ds(0, 63)], a_recv.at[5])
    for half in range(2):
        lanes = slice(half * LANE, (half + 1) * LANE)
        wide = hb[:, half].astype(F32).reshape(BLOCKS * CH, LANE)
        sq_out[:, lanes] = jnp.sum(fold_rows(wide * wide, jnp.sum), axis=0, keepdims=True)
    sq_in[my_chan] = sq_out[...]
    for n in range(1, chan_count):
        send(
            sq_out, sq_in.at[my_chan], o_send.at[8 + n], a_recv.at[6],
            {"chan": (my_chan + n) % chan_count},
        )
    for half in range(2):
        wide = hb[:, half].astype(F32).reshape(BLOCKS * CH, LANE)
        mixed_ref[half * LANE : (half + 1) * LANE, :] = wide.T.astype(BF16)
    if chan_count > 1:
        landed(sq_in.at[pl.ds(0, chan_count - 1)], a_recv.at[6])
    whole = sq_in[0]
    for n in range(1, chan_count):
        whole = whole + sq_in[n]
    inv_out[...] = lax.rsqrt(whole / (BLOCKS * CH * chan_count) + 1e-06)
    others(lambda d: send(inv_out, inv_in.at[me], a_send.at[6], a_recv.at[7], {"seq": d}))
    inv_in[me] = inv_out[...]

    for n in (1, 3, 2):
        slot = row_mates[n] % 8
        landed(kb.at[slot], k_recv.at[slot])
        send(kb.at[slot], kb.at[slot], k_send.at[3 + n], k_recv.at[slot], {"seq": other_core})
    for n in range(4):
        slot = row_mates[n] % 8 + 1 - 2 * core
        landed(kb.at[slot], k_recv.at[slot])

    def scores(slot):
        bq = (my_set + 8 * slot) % SETS

        def tile(t, carry):
            base = tile_base(slot, t)
            q = qb[slot, pl.ds(t * SETS, SETS)].reshape(256, HD)
            qt = q.astype(F32).T.astype(BF16)
            qt_hi = qt[:, LANE:]

            def keys(p):
                return jnp.concatenate(
                    [kb[:, 2 * p].reshape(LANE, HD), kb[:, 2 * p + 1].reshape(LANE, HD)], axis=0
                )

            def plain(u, m):
                for p in (2 * u, 2 * u + 1):
                    s = jnp.dot(keys(p), qt, preferred_element_type=F32)
                    s_ref[p] = s
                    m = jnp.maximum(m, fold_rows(s, jnp.max))
                return m

            def masked(p, width, lane0):
                s = jnp.dot(
                    keys(p), qt if width == 256 else qt_hi, preferred_element_type=F32
                )
                lanes = lax.broadcasted_iota(jnp.int32, (256, width), 1) + lane0
                rows = lax.broadcasted_iota(jnp.int32, (256, width), 0)
                q_pos = (lanes // QR) * ROWS + lanes % QR
                k_pos = (rows // LANE) * ROWS + rows % LANE
                shift = 16 * t * ROWS + bq * QR - 2 * p * ROWS - zr * LANE
                return jnp.where(k_pos - q_pos <= shift, s, -1e30)

            def diag(u, m):
                p = 8 * t + u
                s = masked(p, 256, 0)
                s_ref[p] = s
                return jnp.maximum(m, fold_rows(s, jnp.max))

            def diag_hi(u, m):
                p = 8 * t + 4 + u
                s = masked(p, LANE, LANE)
                s_ref[p, :, LANE:] = s
                return jnp.maximum(m, fold_rows(s, jnp.max))

            m = jnp.full((8, 256), -1e30, F32)
            m = lax.fori_loop(0, 4 * t, plain, m)
            m = lax.fori_loop(0, 4, diag, m, unroll=2)
            m_hi = lax.fori_loop(0, 4, diag_hi, m[:, LANE:], unroll=2)
            m = jnp.concatenate([m[:, :LANE], m_hi], axis=1)
            peak = jnp.max(m, axis=0, keepdims=True)

            def weigh(p, total):
                w = jnp.exp2((s_ref[p] - peak) * factor)
                p_ref[base + p] = w.astype(BF16)
                return total + fold_rows(w, jnp.sum)

            def weigh_two(u, total):
                return weigh(2 * u + 1, weigh(2 * u, total))

            def weigh_hi(u, total):
                p = 8 * t + 4 + u
                w = jnp.exp2((s_ref[p, :, LANE:] - peak[:, LANE:]) * factor)
                p_ref[base + p, :, LANE:] = w.astype(BF16)
                return total + fold_rows(w, jnp.sum)

            total = lax.fori_loop(0, 4 * t + 2, weigh_two, jnp.zeros((8, 256), F32))
            total_hi = lax.fori_loop(0, 4, weigh_hi, total[:, LANE:], unroll=2)
            total = jnp.concatenate([total[:, :LANE], total_hi], axis=1)
            stat[slot, t, :8] = jnp.broadcast_to(peak, (8, 256))
            stat[slot, t, 8:] = jnp.broadcast_to(
                jnp.sum(total, axis=0, keepdims=True), (8, 256)
            )
            return carry

        lax.fori_loop(0, 4, tile, 0)

    def weighted(slot, t):
        base = tile_base(slot, t)

        def both(u, acc):
            for p in (2 * u, 2 * u + 1):
                acc = acc + jnp.dot(vt_ref[p], p_ref[base + p], preferred_element_type=F32)
            return acc

        def high(u, acc):
            p = 8 * t + 4 + u
            return acc + jnp.dot(
                vt_ref[p], p_ref[base + p, :, LANE:], preferred_element_type=F32
            )

        acc = lax.fori_loop(0, 4 * t + 2, both, jnp.zeros((HD, 256), F32))
        acc_hi = lax.fori_loop(0, 4, high, acc[:, LANE:], unroll=2)
        return jnp.concatenate([acc[:, :LANE], acc_hi], axis=1)

    landed(qb.at[1, pl.ds(0, 63)], a_recv.at[3])
    scores(1)
    for n in (4, 1, 3, 5, 7, 2, 6):
        slot = (row_mates[n] if n < 4 else far_mates[n - 4]) % SETS
        landed(vb.at[slot], v_recv.at[slot])
        send(vb.at[slot], vb.at[slot], v_send.at[7 + n], v_recv.at[slot], {"seq": other_core})
    landed(qb.at[0, pl.ds(0, 63)], a_recv.at[4])
    scores(0)

    for n in range(8):
        slot = (row_mates[n] if n < 4 else far_mates[n - 4]) % SETS + 1 - 2 * core
        landed(vb.at[slot], v_recv.at[slot])
    landed(inv_in.at[pl.ds(0, 63)], a_recv.at[7])

    def scale(p, carry):
        for u in range(2):
            v = vb[:, 2 * p + u].astype(F32).reshape(HD, LANE)
            inv = inv_in[2 * p + u, :, pl.ds(pl.multiple_of(zr * LANE, LANE), LANE)]
            vt_ref[p, :, u * LANE : (u + 1) * LANE] = (v * inv).astype(BF16)
        return carry

    lax.fori_loop(0, BLOCKS // 2, scale, 0)

    def help_tile(u, carry):
        t = 3 - u
        acc = weighted(1, t)
        ob_out[t] = (acc / stat[1, t, 8:9]).astype(BF16)
        send(ob_out.at[t], ob_in.at[t], o_send.at[t], o_recv.at[t], {"seq": across})
        send(stat.at[1, t], os_in.at[t], o_send.at[4 + t], o_recv.at[4 + t], {"seq": across})
        return carry

    lax.fori_loop(0, 4, help_tile, 0)

    def own_tile(u, carry):
        t = 3 - u
        acc = weighted(0, t)
        landed(ob_in.at[t], o_recv.at[t])
        landed(os_in.at[t], o_recv.at[4 + t])
        m0, m1 = stat[0, t, 0:1], os_in[t, 0:1]
        top = jnp.maximum(m0, m1)
        w0 = jnp.exp2((m0 - top) * factor)
        w1 = os_in[t, 8:9] * jnp.exp2((m1 - top) * factor)
        total = stat[0, t, 8:9] * w0 + w1
        merged = (acc * w0 + ob_in[t].astype(F32) * w1) / total
        out_ref[pl.ds(pl.multiple_of(t * 256, 256), 256), :] = merged.T.astype(BF16)
        return carry

    lax.fori_loop(0, 4, own_tile, 0)

    landed(rs.at[pl.ds(0, 63)], a_send.at[0])
    landed(kb.at[0, pl.ds(0, 63)], a_send.at[1])
    landed(rg.at[pl.ds(0, 63)], a_send.at[2])
    landed(qb.at[1, pl.ds(0, 63)], a_send.at[3])
    landed(qb.at[0, pl.ds(0, 63)], a_send.at[4])
    landed(hb.at[pl.ds(0, 63)], a_send.at[5])
    landed(inv_in.at[pl.ds(0, 63)], a_send.at[6])
    for n in range(7):
        landed(kb.at[0], k_send.at[n])
    for n in range(15):
        landed(vb.at[0], v_send.at[n])
    for t in range(4):
        landed(ob_in.at[t], o_send.at[t])
        landed(os_in.at[t], o_send.at[4 + t])
    for n in range(1, chan_count):
        landed(sq_in.at[0], o_send.at[8 + n])


def mega_call(sig, gate, taps, skip, q, k):
    return pl.pallas_call(
        mega_kernel,
        out_shape=(
            jax.ShapeDtypeStruct((ROWS, BLOCKS * CH), BF16),
            jax.ShapeDtypeStruct((BLOCKS * QR, HD), BF16),
        ),
        in_specs=[VMEM] * 6,
        out_specs=(VMEM, VMEM),
        scratch_shapes=[
            pltpu.VMEM((BLOCKS, CH, ROWS), BF16),
            pltpu.VMEM((BLOCKS, CH, ROWS), BF16),
            pltpu.VMEM((BLOCKS, CH, ROWS), BF16),
            pltpu.VMEM((BLOCKS, CH, ROWS), BF16),
            pltpu.VMEM((2, BLOCKS, QR, HD), BF16),
            pltpu.VMEM((8, BLOCKS, QR, HD), BF16),
            pltpu.VMEM((2, BLOCKS, CH, LANE), BF16),
            pltpu.VMEM((BLOCKS, 2, CH, LANE), BF16),
            pltpu.VMEM((SETS, BLOCKS, CH, LANE), BF16),
            pltpu.VMEM((1, ROWS), F32),
            pltpu.VMEM((4, 1, ROWS), F32),
            pltpu.VMEM((1, ROWS), F32),
            pltpu.VMEM((BLOCKS, 1, ROWS), F32),
            pltpu.VMEM((BLOCKS * ROWS, ROWS), BF16),
            pltpu.VMEM((576, ROWS), F32),
            pltpu.VMEM((512, 2048), BF16),
            pltpu.VMEM((512, ROWS), F32),
            pltpu.VMEM((BLOCKS // 2, 256, 256), F32),
            pltpu.VMEM((160, 256, 256), BF16),
            pltpu.VMEM((BLOCKS // 2, HD, 256), BF16),
            pltpu.VMEM((2, 4, 16, 256), F32),
            pltpu.VMEM((4, HD, 256), BF16),
            pltpu.VMEM((4, HD, 256), BF16),
            pltpu.VMEM((4, 16, 256), F32),
            pltpu.VMEM((4, 16, 256), F32),
            pltpu.SemaphoreType.DMA((7,)),
            pltpu.SemaphoreType.DMA((8,)),
            pltpu.SemaphoreType.DMA((7,)),
            pltpu.SemaphoreType.DMA((8,)),
            pltpu.SemaphoreType.DMA((15,)),
            pltpu.SemaphoreType.DMA((16,)),
            pltpu.SemaphoreType.DMA((12,)),
            pltpu.SemaphoreType.DMA((8,)),
        ],
        compiler_params=pltpu.CompilerParams(
            vmem_limit_bytes=62 * 2**20, collective_id=0, has_side_effects=True
        ),
        name="mega",
    )(sig, gate, taps, skip, q, k)


def shards(signal, gate_rows, skip_gain, filter_taps, queries, key_rows):
    me = lax.axis_index("seq")
    taps = lax.dynamic_slice_in_dim(filter_taps.T, me // SETS, 1, 0)
    taps = taps.reshape(LANE, LANE).astype(F32)
    skip = jnp.broadcast_to(lax.dynamic_slice_in_dim(skip_gain, me * CH, CH)[:, None], (CH, ROWS))
    mixed, attended = mega_call(signal, gate_rows, taps, skip, queries, key_rows)
    return mixed, attended[None]


def solution(mesh):
    in_specs = (
        P("seq", "chan"),
        P("seq", "chan"),
        P("chan"),
        P(None, "chan"),
        P("seq", "chan"),
        P("seq", "chan"),
    )
    out_specs = (P("seq", "chan"), P(("chan", "seq"), None, None))
    return jax.shard_map(shards, mesh=mesh, in_specs=in_specs, out_specs=out_specs, check_vma=False)
```

time: 203 us -> 108 us (0.53)
  blocking collectives: 101 us -> 0 us
  Pallas kernels: 51.3 us -> 100 us
  waiting for transfers between devices: 15.9 us -> 0 us
  between operations: 14.1 us -> 0.67 us
  starting transfers between devices: 13.2 us -> 0 us
    pallas_call x2 -> x1, Pallas kernels: 51.3 us -> 100 us  [mega_call(): pl.pallas_call(mega_kernel, out_shape=(jax.ShapeDtypeStruct((ROWS, BLOCKS...]
    all_to_all x2 -> x0, blocking collectives: 47.2 us -> none  [the longest x1 25.7 us: shards(): qk = lax.all_to_all(qk, 'seq', split_axis=0, concat_axis=0, tiled=True)]
    all_gather x1 -> x0, blocking collectives: 45.6 us -> none  [shards(): inv_all = lax.all_gather(inv, 'seq', axis=0, tiled=False)]
    all_to_all x1 -> x0, waiting for transfers between devices: 15.9 us -> none  [shards(): sg = lax.all_to_all(sg, 'seq', split_axis=0, concat_axis=0, tiled=True)]
    all_to_all x1 -> x0, starting transfers between devices: 13.1 us -> none  [shards(): sg = lax.all_to_all(sg, 'seq', split_axis=0, concat_axis=0, tiled=True)]
    psum x1 -> x0, blocking collectives: 8.58 us -> none  [shards(): whole = lax.psum(squares, 'chan')]
    unnamed x5 -> x4, local copies, waits for them, and re-layouts: 0.01 us -> 2.42 us
    transpose x2 -> x0, local copies, waits for them, and re-layouts: 2.22 us -> none  [split_channels(): return x.T.reshape(BLOCKS, 1, CH, ROWS)]
  transfers between devices with their start and end apart: 3 -> 0, of which waited for: 1 -> 0; matrix products, arithmetic and copies ran while one was open for 2% -> 0% of each run, Pallas kernels for 0% -> 0%
where the time goes in v2:
time: 108 us; the launch traced here: 107 us
  Pallas kernels  100 us (93%)
  local copies, waits for them, and re-layouts  3.85 us (4%)
  other arithmetic  1.59 us (1%)
    pallas_call x1, Pallas kernels, mega_call(): pl.pallas_call(mega_kernel, out_shape=(jax.ShapeDtypeStruct((ROWS, BLOCKS...  100 us
    unnamed x4, local copies, waits for them, and re-layouts  2.42 us

profile of v2, /device:TPU:1, one launch (start us, length us, event | category | flops | bytes accessed | tf_op | source)
XLA Modules:
  0.0 106.5 jit_solution(6985189407657652332)
XLA Ops:
  0.6 0.8 dynamic_slice.4
  1.4 0.7 broadcast_in_dim.4.skip_ref
  2.1 1.6 %dynamic-slice_convert_fusion = f32[16384,1]{0,1:T(1,128)} fusion(bf16[16384,4]{0,1:T(4,128)(2,1)} %param.9, s32[]{:T(128)S(6)} %select_n.12), kind=kLoop, calls=%fused_computation | loop fusion | flops 16384 | bytes 98308 | tf_op jit(solution)/shard_map/convert_element_type | solution.py:427
  3.7 100.4 %mega.1 = (bf16[256,512]{1,0:T(8,128)(2,1)}, bf16[1024,128]{1,0:T(8,128)(2,1)}) custom-call(bf16[256,512]{1,0:T(8,128)(2,1)} %sig_ref.1, bf16[256,512]{1,0:T(8,128)(2,1)} %gate_ref.1, f32[128,128]{1,0:T(8,128)} %bitcast.2, f32[8,256]{1,0:T(8,128)} %broadcast_in_dim.4.skip_ref, bf16[256,512]{1,0:T(8,128)(2,1)} %q_ref.1, bf16[256,512]{1,0:T(8,128)(2,1)} %k_ref.1), custom_call_target="tpu_custom_call" | custom-call | tf_op jit(solution)/shard_map/mega/pallas_call | solution.py:374
  104.1 0.0 copy-start
  104.1 1.7 %copy.10 = bf16[256,512]{1,0:T(8,128)(2,1)} copy(bf16[256,512]{1,0:T(8,128)(2,1)} %get-tuple-element.8) | data formatting | bytes 524288
  105.8 0.0 copy-done
  105.8 0.7 copy.11
Async XLA Ops:
  104.1 1.7 %copy-start = (bf16[1024,128]{1,0:T(8,128)(2,1)S(1)}, bf16[1024,128]{1,0:T(8,128)(2,1)}, u32[]{:S(2)}) copy-start(bf16[1024,128]{1,0:T(8,128)(2,1)} %get-tuple-element.5) | copy-start | bytes 786436

commit v3 on v2

--- a/solution.py
+++ b/solution.py
@@ -99,9 +99,6 @@
         rows = pl.ds(pl.multiple_of((d % SETS) * QR, QR), QR)
         return ref.at[rows, pl.ds(pl.multiple_of((d // SETS) * HD, HD), HD)]
 
-    def flip(d):
-        return d + 8 - 16 * ((d // 8) % 2)
-
     st_s[...] = sig_ref[...].astype(F32).T.reshape(BLOCKS, CH, ROWS).astype(BF16)
     st_g[...] = gate_ref[...].astype(F32).T.reshape(BLOCKS, CH, ROWS).astype(BF16)
 
@@ -125,16 +122,15 @@
     )
     others(lambda d: send(st_g.at[d], rg.at[me], a_send.at[2], a_recv.at[2], {"seq": d}))
 
-    def send_queries(d):
-        send(piece(q_ref, flip(d)), qb.at[1, me], a_send.at[3], a_recv.at[3], {"seq": d})
-        send(piece(q_ref, d), qb.at[0, me], a_send.at[4], a_recv.at[4], {"seq": d})
-
-    others(send_queries)
+    others(
+        lambda d: send(
+            piece(q_ref, d), qb.at[0, me], a_send.at[4], a_recv.at[4], {"seq": d}
+        )
+    )
     rs[me] = st_s[me]
     rg[me] = st_g[me]
     kb[my_slot, me] = piece(k_ref, me)[...]
     qb[0, me] = piece(q_ref, me)[...]
-    qb[1, me] = piece(q_ref, across)[...]
 
     fill_toeplitz(taps_ref, gg)
     xf[:64, :] = jnp.zeros((64, ROWS), F32)
@@ -168,15 +164,122 @@
     cmh[1] = mixed[:, :, LANE:]
     others(lambda d: send(cmh.at[:, d], hb.at[me], a_send.at[5], a_recv.at[5], {"seq": d}))
     hb[me] = cmh[:, me]
+    send(cmh.at[1 - zr], vb.at[my_set], v_send.at[4], v_recv.at[my_set], {"seq": across})
     vb[my_set] = cmh[zr]
     for n in range(4):
         where = other_core if n == 0 else row_mates[n]
         send(cmh.at[zr], vb.at[my_set], v_send.at[n], v_recv.at[my_set], {"seq": where})
+
+    for n in (1, 3, 2):
+        slot = row_mates[n] % 8
+        landed(kb.at[slot], k_recv.at[slot])
+        send(kb.at[slot], kb.at[slot], k_send.at[3 + n], k_recv.at[slot], {"seq": other_core})
     for n in range(4):
-        send(
-            cmh.at[1 - zr], vb.at[my_set], v_send.at[4 + n], v_recv.at[my_set],
-            {"seq": far_mates[n]},
-        )
+        slot = row_mates[n] % 8 + 1 - 2 * core
+        landed(kb.at[slot], k_recv.at[slot])
+
+    def scores(slot, first, last):
+        bq = (my_set + 8 * slot) % SETS
+
+        def tile(t, carry):
+            base = tile_base(slot, t)
+            q = qb[slot, pl.ds(t * SETS, SETS)].reshape(256, HD)
+            qt = q.astype(F32).T.astype(BF16)
+            qt_hi = qt[:, LANE:]
+
+            def keys(p):
+                return jnp.concatenate(
+                    [kb[:, 2 * p].reshape(LANE, HD), kb[:, 2 * p + 1].reshape(LANE, HD)], axis=0
+                )
+
+            def plain(u, m):
+                for p in (2 * u, 2 * u + 1):
+                    s = jnp.dot(keys(p), qt, preferred_element_type=F32)
+                    s_ref[p] = s
+                    m = jnp.maximum(m, fold_rows(s, jnp.max))
+                return m
+
+            def masked(p, width, lane0):
+                s = jnp.dot(
+                    keys(p), qt if width == 256 else qt_hi, preferred_element_type=F32
+                )
+                lanes = lax.broadcasted_iota(jnp.int32, (256, width), 1) + lane0
+                rows = lax.broadcasted_iota(jnp.int32, (256, width), 0)
+                q_pos = (lanes // QR) * ROWS + lanes % QR
+                k_pos = (rows // LANE) * ROWS + rows % LANE
+                shift = 16 * t * ROWS + bq * QR - 2 * p * ROWS - zr * LANE
+                return jnp.where(k_pos - q_pos <= shift, s, -1e30)
+
+            def diag(u, m):
+                p = 8 * t + u
+                s = masked(p, 256, 0)
+                s_ref[p] = s
+                return jnp.maximum(m, fold_rows(s, jnp.max))
+
+            def diag_hi(u, m):
+                p = 8 * t + 4 + u
+                s = masked(p, LANE, LANE)
+                s_ref[p, :, LANE:] = s
+                return jnp.maximum(m, fold_rows(s, jnp.max))
+
+            m = jnp.full((8, 256), -1e30, F32)
+            m = lax.fori_loop(0, 4 * t, plain, m)
+            m = lax.fori_loop(0, 4, diag, m, unroll=2)
+            m_hi = lax.fori_loop(0, 4, diag_hi, m[:, LANE:], unroll=2)
+            m = jnp.concatenate([m[:, :LANE], m_hi], axis=1)
+            peak = jnp.max(m, axis=0, keepdims=True)
+
+            def weigh(p, total):
+                w = jnp.exp2((s_ref[p] - peak) * factor)
+                p_ref[base + p] = w.astype(BF16)
+                return total + fold_rows(w, jnp.sum)
+
+            def weigh_two(u, total):
+                return weigh(2 * u + 1, weigh(2 * u, total))
+
+            def weigh_hi(u, total):
+                p = 8 * t + 4 + u
+                w = jnp.exp2((s_ref[p, :, LANE:] - peak[:, LANE:]) * factor)
+                p_ref[base + p, :, LANE:] = w.astype(BF16)
+                return total + fold_rows(w, jnp.sum)
+
+            total = lax.fori_loop(0, 4 * t + 2, weigh_two, jnp.zeros((8, 256), F32))
+            total_hi = lax.fori_loop(0, 4, weigh_hi, total[:, LANE:], unroll=2)
+            total = jnp.concatenate([total[:, :LANE], total_hi], axis=1)
+            stat[slot, t, :8] = jnp.broadcast_to(peak, (8, 256))
+            stat[slot, t, 8:] = jnp.broadcast_to(
+                jnp.sum(total, axis=0, keepdims=True), (8, 256)
+            )
+            return carry
+
+        lax.fori_loop(first, last, tile, 0)
+
+    def weighted(slot, t):
+        base = tile_base(slot, t)
+
+        def both(u, acc):
+            for p in (2 * u, 2 * u + 1):
+                acc = acc + jnp.dot(vt_ref[p], p_ref[base + p], preferred_element_type=F32)
+            return acc
+
+        def high(u, acc):
+            p = 8 * t + 4 + u
+            return acc + jnp.dot(
+                vt_ref[p], p_ref[base + p, :, LANE:], preferred_element_type=F32
+            )
+
+        acc = lax.fori_loop(0, 4 * t + 2, both, jnp.zeros((HD, 256), F32))
+        acc_hi = lax.fori_loop(0, 4, high, acc[:, LANE:], unroll=2)
+        return jnp.concatenate([acc[:, :LANE], acc_hi], axis=1)
+
+    def pass_values(n):
+        slot = (row_mates[n] if n < 4 else far_mates[n - 4]) % SETS
+        landed(vb.at[slot], v_recv.at[slot])
+        send(vb.at[slot], vb.at[slot], v_send.at[8 + n - n // 4], v_recv.at[slot], {"seq": other_core})
+
+    landed(qb.at[0, pl.ds(0, 63)], a_recv.at[4])
+    send(qb.at[0], qb.at[1], a_send.at[3], a_recv.at[3], {"seq": across})
+    scores(0, 0, 3)
 
     landed(hb.at[pl.ds(0, 63)], a_recv.at[5])
     for half in range(2):
@@ -192,6 +295,14 @@
     for half in range(2):
         wide = hb[:, half].astype(F32).reshape(BLOCKS * CH, LANE)
         mixed_ref[half * LANE : (half + 1) * LANE, :] = wide.T.astype(BF16)
+
+    far = across % SETS
+    landed(vb.at[far], v_recv.at[far])
+    for n in (1, 3, 2):
+        send(vb.at[far], vb.at[far], v_send.at[4 + n], v_recv.at[far], {"seq": row_mates[n]})
+    send(vb.at[far], vb.at[far], v_send.at[8], v_recv.at[far], {"seq": other_core})
+    scores(0, 3, 4)
+
     if chan_count > 1:
         landed(sq_in.at[pl.ds(0, chan_count - 1)], a_recv.at[6])
     whole = sq_in[0]
@@ -202,115 +313,12 @@
     inv_in[me] = inv_out[...]
 
     for n in (1, 3, 2):
-        slot = row_mates[n] % 8
-        landed(kb.at[slot], k_recv.at[slot])
-        send(kb.at[slot], kb.at[slot], k_send.at[3 + n], k_recv.at[slot], {"seq": other_core})
-    for n in range(4):
-        slot = row_mates[n] % 8 + 1 - 2 * core
-        landed(kb.at[slot], k_recv.at[slot])
-
-    def scores(slot):
-        bq = (my_set + 8 * slot) % SETS
-
-        def tile(t, carry):
-            base = tile_base(slot, t)
-            q = qb[slot, pl.ds(t * SETS, SETS)].reshape(256, HD)
-            qt = q.astype(F32).T.astype(BF16)
-            qt_hi = qt[:, LANE:]
-
-            def keys(p):
-                return jnp.concatenate(
-                    [kb[:, 2 * p].reshape(LANE, HD), kb[:, 2 * p + 1].reshape(LANE, HD)], axis=0
-                )
-
-            def plain(u, m):
-                for p in (2 * u, 2 * u + 1):
-                    s = jnp.dot(keys(p), qt, preferred_element_type=F32)
-                    s_ref[p] = s
-                    m = jnp.maximum(m, fold_rows(s, jnp.max))
-                return m
-
-            def masked(p, width, lane0):
-                s = jnp.dot(
-                    keys(p), qt if width == 256 else qt_hi, preferred_element_type=F32
-                )
-                lanes = lax.broadcasted_iota(jnp.int32, (256, width), 1) + lane0
-                rows = lax.broadcasted_iota(jnp.int32, (256, width), 0)
-                q_pos = (lanes // QR) * ROWS + lanes % QR
-                k_pos = (rows // LANE) * ROWS + rows % LANE
-                shift = 16 * t * ROWS + bq * QR - 2 * p * ROWS - zr * LANE
-                return jnp.where(k_pos - q_pos <= shift, s, -1e30)
-
-            def diag(u, m):
-                p = 8 * t + u
-                s = masked(p, 256, 0)
-                s_ref[p] = s
-                return jnp.maximum(m, fold_rows(s, jnp.max))
-
-            def diag_hi(u, m):
-                p = 8 * t + 4 + u
-                s = masked(p, LANE, LANE)
-                s_ref[p, :, LANE:] = s
-                return jnp.maximum(m, fold_rows(s, jnp.max))
-
-            m = jnp.full((8, 256), -1e30, F32)
-            m = lax.fori_loop(0, 4 * t, plain, m)
-            m = lax.fori_loop(0, 4, diag, m, unroll=2)
-            m_hi = lax.fori_loop(0, 4, diag_hi, m[:, LANE:], unroll=2)
-            m = jnp.concatenate([m[:, :LANE], m_hi], axis=1)
-            peak = jnp.max(m, axis=0, keepdims=True)
-
-            def weigh(p, total):
-                w = jnp.exp2((s_ref[p] - peak) * factor)
-                p_ref[base + p] = w.astype(BF16)
-                return total + fold_rows(w, jnp.sum)
-
-            def weigh_two(u, total):
-                return weigh(2 * u + 1, weigh(2 * u, total))
-
-            def weigh_hi(u, total):
-                p = 8 * t + 4 + u
-                w = jnp.exp2((s_ref[p, :, LANE:] - peak[:, LANE:]) * factor)
-                p_ref[base + p, :, LANE:] = w.astype(BF16)
-                return total + fold_rows(w, jnp.sum)
-
-            total = lax.fori_loop(0, 4 * t + 2, weigh_two, jnp.zeros((8, 256), F32))
-            total_hi = lax.fori_loop(0, 4, weigh_hi, total[:, LANE:], unroll=2)
-            total = jnp.concatenate([total[:, :LANE], total_hi], axis=1)
-            stat[slot, t, :8] = jnp.broadcast_to(peak, (8, 256))
-            stat[slot, t, 8:] = jnp.broadcast_to(
-                jnp.sum(total, axis=0, keepdims=True), (8, 256)
-            )
-            return carry
-
-        lax.fori_loop(0, 4, tile, 0)
-
-    def weighted(slot, t):
-        base = tile_base(slot, t)
-
-        def both(u, acc):
-            for p in (2 * u, 2 * u + 1):
-                acc = acc + jnp.dot(vt_ref[p], p_ref[base + p], preferred_element_type=F32)
-            return acc
-
-        def high(u, acc):
-            p = 8 * t + 4 + u
-            return acc + jnp.dot(
-                vt_ref[p], p_ref[base + p, :, LANE:], preferred_element_type=F32
-            )
-
-        acc = lax.fori_loop(0, 4 * t + 2, both, jnp.zeros((HD, 256), F32))
-        acc_hi = lax.fori_loop(0, 4, high, acc[:, LANE:], unroll=2)
-        return jnp.concatenate([acc[:, :LANE], acc_hi], axis=1)
-
-    landed(qb.at[1, pl.ds(0, 63)], a_recv.at[3])
-    scores(1)
-    for n in (4, 1, 3, 5, 7, 2, 6):
-        slot = (row_mates[n] if n < 4 else far_mates[n - 4]) % SETS
-        landed(vb.at[slot], v_recv.at[slot])
-        send(vb.at[slot], vb.at[slot], v_send.at[7 + n], v_recv.at[slot], {"seq": other_core})
-    landed(qb.at[0, pl.ds(0, 63)], a_recv.at[4])
-    scores(0)
+        pass_values(n)
+    landed(qb.at[1], a_recv.at[3])
+    scores(1, 0, 3)
+    for n in (5, 7, 6):
+        pass_values(n)
+    scores(1, 3, 4)
 
     for n in range(8):
         slot = (row_mates[n] if n < 4 else far_mates[n - 4]) % SETS + 1 - 2 * core
@@ -355,7 +363,7 @@
     landed(rs.at[pl.ds(0, 63)], a_send.at[0])
     landed(kb.at[0, pl.ds(0, 63)], a_send.at[1])
     landed(rg.at[pl.ds(0, 63)], a_send.at[2])
-    landed(qb.at[1, pl.ds(0, 63)], a_send.at[3])
+    landed(qb.at[0], a_send.at[3])
     landed(qb.at[0, pl.ds(0, 63)], a_send.at[4])
     landed(hb.at[pl.ds(0, 63)], a_send.at[5])
     landed(inv_in.at[pl.ds(0, 63)], a_send.at[6])

time: 108 us -> 99.5 us (0.921); the launches traced: 107 us -> 99.4 us
  Pallas kernels: 100 us -> 93.2 us
    pallas_call x1, Pallas kernels: 100 us -> 93.2 us  [mega_call(): pl.pallas_call(mega_kernel, out_shape=(jax.ShapeDtypeStruct((ROWS, BLOCKS...]
where the time goes in v3:
time: 99.5 us; the launch traced here: 99.4 us
  Pallas kernels  93.2 us (94%)
  local copies, waits for them, and re-layouts  3.85 us (4%)
  other arithmetic  1.59 us (2%)
    pallas_call x1, Pallas kernels, mega_call(): pl.pallas_call(mega_kernel, out_shape=(jax.ShapeDtypeStruct((ROWS, BLOCKS...  93.2 us
    unnamed x4, local copies, waits for them, and re-layouts  2.42 us

profile of v3, /device:TPU:1, one launch (start us, length us, event | category | flops | bytes accessed | tf_op | source)
XLA Modules:
  0.0 99.4 jit_solution(9166422485737438866)
XLA Ops:
  0.6 0.8 dynamic_slice.4
  1.4 0.7 broadcast_in_dim.4.skip_ref
  2.1 1.6 %dynamic-slice_convert_fusion = f32[16384,1]{0,1:T(1,128)} fusion(bf16[16384,4]{0,1:T(4,128)(2,1)} %param.9, s32[]{:T(128)S(6)} %select_n.12), kind=kLoop, calls=%fused_computation | loop fusion | flops 16384 | bytes 98308 | tf_op jit(solution)/shard_map/convert_element_type | solution.py:435
  3.7 93.2 %mega.1 = (bf16[256,512]{1,0:T(8,128)(2,1)}, bf16[1024,128]{1,0:T(8,128)(2,1)}) custom-call(bf16[256,512]{1,0:T(8,128)(2,1)} %sig_ref.1, bf16[256,512]{1,0:T(8,128)(2,1)} %gate_ref.1, f32[128,128]{1,0:T(8,128)} %bitcast.2, f32[8,256]{1,0:T(8,128)} %broadcast_in_dim.4.skip_ref, bf16[256,512]{1,0:T(8,128)(2,1)} %q_ref.1, bf16[256,512]{1,0:T(8,128)(2,1)} %k_ref.1), custom_call_target="tpu_custom_call" | custom-call | tf_op jit(solution)/shard_map/mega/pallas_call | solution.py:382
  96.9 0.0 copy-start
  96.9 1.7 %copy.10 = bf16[256,512]{1,0:T(8,128)(2,1)} copy(bf16[256,512]{1,0:T(8,128)(2,1)} %get-tuple-element.8) | data formatting | bytes 524288
  98.6 0.0 copy-done
  98.6 0.7 copy.11
Async XLA Ops:
  96.9 1.7 %copy-start = (bf16[1024,128]{1,0:T(8,128)(2,1)S(1)}, bf16[1024,128]{1,0:T(8,128)(2,1)}, u32[]{:S(2)}) copy-start(bf16[1024,128]{1,0:T(8,128)(2,1)} %get-tuple-element.5) | copy-start | bytes 786436

commit v4 on v3

--- a/solution.py
+++ b/solution.py
@@ -158,7 +158,12 @@
 
     landed(rg.at[pl.ds(0, 63)], a_recv.at[2])
     conv = acc_ref[...].reshape(BLOCKS, CH, ROWS)
-    mixed = rg[...].astype(F32) * (conv + skip_ref[...][None] * rs[...].astype(F32))
+    lane = lax.broadcasted_iota(jnp.int32, (CH, BLOCKS * CH), 1)
+    row = lax.broadcasted_iota(jnp.int32, (CH, BLOCKS * CH), 0)
+    gains = jnp.broadcast_to(skip_ref[...], (CH, BLOCKS * CH))
+    gains = jnp.sum(jnp.where(lane == me * CH + row, gains, 0.0), axis=1, keepdims=True)
+    gains = jnp.broadcast_to(gains, (CH, ROWS))
+    mixed = rg[...].astype(F32) * (conv + gains[None] * rs[...].astype(F32))
     mixed = mixed.astype(BF16)
     cmh[0] = mixed[:, :, :LANE]
     cmh[1] = mixed[:, :, LANE:]
@@ -433,7 +438,7 @@
     me = lax.axis_index("seq")
     taps = lax.dynamic_slice_in_dim(filter_taps.T, me // SETS, 1, 0)
     taps = taps.reshape(LANE, LANE).astype(F32)
-    skip = jnp.broadcast_to(lax.dynamic_slice_in_dim(skip_gain, me * CH, CH)[:, None], (CH, ROWS))
+    skip = skip_gain.reshape(1, BLOCKS * CH)
     mixed, attended = mega_call(signal, gate_rows, taps, skip, queries, key_rows)
     return mixed, attended[None]
 

time: 99.5 us -> 98.3 us (0.988)
  local copies, waits for them, and re-layouts: 3.85 us -> 2.42 us
where the time goes in v4:
time: 98.3 us; the launch traced here: 97.9 us
  Pallas kernels  93.2 us (95%)
  local copies, waits for them, and re-layouts  2.42 us (2%)
  other arithmetic  1.6 us (2%)
    pallas_call x1, Pallas kernels, mega_call(): pl.pallas_call(mega_kernel, out_shape=(jax.ShapeDtypeStruct((ROWS, BLOCKS...  93.2 us
    unnamed x4, local copies, waits for them, and re-layouts  2.42 us

profile of v4, /device:TPU:1, one launch (start us, length us, event | category | flops | bytes accessed | tf_op | source)
XLA Modules:
  0.0 97.9 jit_solution(16406602763570848353)
XLA Ops:
  0.6 1.6 %dynamic-slice_convert_fusion = f32[16384,1]{0,1:T(1,128)} fusion(bf16[16384,4]{0,1:T(4,128)(2,1)} %param.9, s32[]{:T(128)S(6)} %select_n.9), kind=kLoop, calls=%fused_computation | loop fusion | flops 16384 | bytes 98308 | tf_op jit(solution)/shard_map/convert_element_type | solution.py:440
  2.2 93.2 %mega.1 = (bf16[256,512]{1,0:T(8,128)(2,1)}, bf16[1024,128]{1,0:T(8,128)(2,1)}) custom-call(bf16[256,512]{1,0:T(8,128)(2,1)} %sig_ref.1, bf16[256,512]{1,0:T(8,128)(2,1)} %gate_ref.1, f32[128,128]{1,0:T(8,128)} %bitcast.3, f32[1,512]{1,0:T(1,128)} %bitcast.5, bf16[256,512]{1,0:T(8,128)(2,1)} %q_ref.1, bf16[256,512]{1,0:T(8,128)(2,1)} %k_ref.1), custom_call_target="tpu_custom_call" | custom-call | tf_op jit(solution)/shard_map/mega/pallas_call | solution.py:387
  95.5 0.0 copy-start
  95.5 1.7 %copy.10 = bf16[256,512]{1,0:T(8,128)(2,1)} copy(bf16[256,512]{1,0:T(8,128)(2,1)} %get-tuple-element.8) | data formatting | bytes 524288
  97.2 0.0 copy-done
  97.2 0.7 copy.11
Async XLA Ops:
  95.5 1.7 %copy-start = (bf16[1024,128]{1,0:T(8,128)(2,1)S(1)}, bf16[1024,128]{1,0:T(8,128)(2,1)}, u32[]{:S(2)}) copy-start(bf16[1024,128]{1,0:T(8,128)(2,1)} %get-tuple-element.5) | copy-start | bytes 786436
